TPU v7x, 32 devices: a whole 2x2x4 slice. The times are simulated.
32 devices in a mesh: row: 8 (over y, x, core), col: 4 (over z).
Axes of the slice: x: 2, y: 2, z: 4, core: 2. Of those that a mesh axis runs over, the one named last changes fastest.
Arguments:
- attn_out: bfloat16 [2, 256, 16384], P(None, 'row', 'col'), may hold values from -6 to 6
- o_weight: bfloat16 [16384, 16384], P('col', 'row'), may hold values from -0.046875 to 0.046875
- residual: float32 [2, 256, 16384], P(None, 'col', 'row'), may hold values from -73 to 73
- norm_gain: float32 [16384], replicated, may hold values from 0.5 to 1.5
- gram_in: float32 [16384, 16384], P('row', 'col'), may hold values from -0.1 to 1.5
Outputs:
- gram: float32 [16384, 16384], P('row', 'col')
All inputs are finite; a program needn't handle non-finite values.
Results may differ from a plain program's by a relative error of at most 0.0003.
Values may be sent and summed in bfloat16 or wider, within the bound.
A program may use at most 192 MiB of HBM per device.

v0:
```python
import jax
import jax.numpy as jnp
from jax import lax
from jax.sharding import PartitionSpec as P

epsilon_norm = 1e-05
highest = lax.Precision.HIGHEST


def spread(block, axis, owner):
    block = jnp.where(lax.axis_index(axis) == owner, block, jnp.zeros_like(block))
    return lax.psum(block, axis)


def outer_sum(left_rows, right_rows):
    return lax.dot_general(
        left_rows,
        right_rows,
        (((0,), (0,)), ((), ())),
        precision=highest,
        preferred_element_type=jnp.float32,
    )


def body(attn_out, o_weight, residual, norm_gain, gram_in):
    row_count = lax.axis_size("row")
    col_count = lax.axis_size("col")
    fan_ratio = row_count // col_count
    row_index = lax.axis_index("row")
    col_index = lax.axis_index("col")
    col_width = o_weight.shape[0]
    row_width = o_weight.shape[1]
    model_width = row_width * row_count
    group_tokens = attn_out.shape[1] * row_count
    local_tokens = residual.shape[1]
    gain_rows = lax.dynamic_slice_in_dim(norm_gain, row_index * row_width, row_width)
    gram_sum = jnp.zeros((row_width, col_width), jnp.float32)
    for block_index in range(attn_out.shape[0]):
        resid_block = residual[block_index]
        partial_value = jnp.dot(
            lax.all_gather(attn_out[block_index], "row", axis=0, tiled=True),
            o_weight,
            preferred_element_type=jnp.float32,
        )
        offset = col_index * local_tokens
        own_rows = lax.dynamic_slice_in_dim(partial_value, offset, local_tokens, 0) + resid_block
        partial_value = lax.dynamic_update_slice_in_dim(partial_value, own_rows, offset, 0)
        row_panel = lax.psum(partial_value, "col")
        panel_sums = lax.psum(jnp.sum(row_panel * row_panel, axis=1), "row")
        inverse_rms = lax.rsqrt(panel_sums / model_width + epsilon_norm)
        row_panel = row_panel * inverse_rms[:, None] * gain_rows[None, :]
        column_parts = []
        for member in range(fan_ratio):
            column_parts.append(spread(row_panel, "row", col_index * fan_ratio + member))
        column_block = jnp.concatenate(column_parts, axis=1)
        gram_sum = gram_sum + outer_sum(row_panel, column_block)
    return gram_in + gram_sum / (attn_out.shape[0] * group_tokens)


def solution(mesh):
    return jax.shard_map(
        body,
        mesh=mesh,
        in_specs=(
            P(None, "row", "col"),
            P("col", "row"),
            P(None, "col", "row"),
            P(),
            P("row", "col"),
        ),
        out_specs=P("row", "col"),
        check_vma=False,
    )
```

profile of v0, /device:TPU:5, one launch (start us, length us, event | category | flops | bytes accessed | tf_op | source)
XLA Modules:
  0.0 464.3 jit_solution(1088472988798540097)
XLA Ops:
  6.5 0.0 all-gather.7.cloned.1.call-start
  6.5 1.8 fusion.23
  8.4 0.0 all-gather.7.cloned.1.call-update
  8.4 0.0 all-gather.5.cloned.1.call-start
  8.5 0.7 all-gather.5.cloned.1.call-update
  9.2 0.0 all-reduce.8.cloned.1.call-start
  9.2 29.3 %all-gather.7.cloned.1.call-done = bf16[1,256,4096]{2,1,0:T(8,128)(2,1)} async-done(((bf16[1,32,4096]{2,1,0:T(8,128)(2,1)}), bf16[1,256,4096]{2,1,0:T(8,128)(2,1)}) %all-gather.7.cloned.1.call-update) | async-done | bytes 2097168 | tf_op jit(solution)/shard_map/all_gather | solution.py:41
  38.6 8.7 %fusion.7 = f32[256,2048]{1,0:T(8,128)S(1)} fusion(bf16[4096,2048]{1,0:T(8,128)(2,1)} %param.6, bf16[1,256,4096]{2,1,0:T(8,128)(2,1)} %all-gather.7.cloned.1.call-done), kind=kOutput, calls=%fused_computation.8 | convolution fusion | flops 4294967296 | bytes 20971520 | tf_op jit(solution)/shard_map/dot_general | solution.py:40
  47.3 0.0 copy-start.3
  47.3 21.0 %all-gather.5.cloned.1.call-done = bf16[1,256,4096]{2,1,0:T(8,128)(2,1)} async-done(((bf16[1,32,4096]{2,1,0:T(8,128)(2,1)}), bf16[1,256,4096]{2,1,0:T(8,128)(2,1)}) %all-gather.5.cloned.1.call-update) | async-done | bytes 2097168 | tf_op jit(solution)/shard_map/all_gather | solution.py:41
  68.3 8.7 %fusion.9 = f32[256,2048]{1,0:T(8,128)S(1)} fusion(bf16[4096,2048]{1,0:T(8,128)(2,1)} %param.6, bf16[1,256,4096]{2,1,0:T(8,128)(2,1)} %all-gather.5.cloned.1.call-done), kind=kOutput, calls=%fused_computation.10 | convolution fusion | flops 4294967296 | bytes 20971520 | tf_op jit(solution)/shard_map/dot_general | solution.py:40
  77.0 0.0 copy-done.3
  77.0 0.2 fusion.19
  77.2 0.0 copy-start.2
  77.2 1.3 copy-done.2
  78.5 0.0 copy-start.1
  78.5 1.3 copy-done.1
  79.9 0.0 all-reduce.8.cloned.1.call-update
  79.9 0.0 all-reduce.6.cloned.1.call-start
  80.0 0.7 dynamic_slice.10
  80.7 153.9 %all-reduce.8.cloned.1.call-done = (f32[256,2048]{1,0:T(8,128)}, f32[256,2048]{1,0:T(8,128)}) async-done(((f32[256,2048]{1,0:T(8,128)}, f32[256,2048]{1,0:T(8,128)}), (f32[256,2048]{1,0:T(8,128)}, f32[256,2048]{1,0:T(8,128)})) %all-reduce.8.cloned.1.call-update) | async-done | bytes 4194320 | tf_op jit(solution)/shard_map/psum | solution.py:48
  234.6 0.0 copy-start
  234.6 2.7 multiply_reduce_fusion
  237.3 12.2 %all-reduce = (f32[256]{0:T(256)S(1)}, f32[256]{0:T(256)S(1)}) all-reduce(f32[256]{0:T(256)S(1)} %get-tuple-element.24, f32[256]{0:T(256)S(1)} %get-tuple-element.23), channel_id=1, replica_groups=mesh['row'=8,'col'=4] {'row'}, use_global_device_ids=true, to_apply=%region_2.0 | all-reduce | flops 512 | bytes 4096 | tf_op jit(solution)/shard_map/psum | solution.py:49
  249.5 0.0 copy-done
  249.5 5.4 %fusion.14 = (f32[256,2048]{1,0:T(8,128)}, f32[256,2048]{1,0:T(8,128)}, f32[256,2048]{1,0:T(8,128)}, f32[256,2048]{1,0:T(8,128)}) fusion(f32[256,2048]{1,0:T(8,128)} %get-tuple-element.12, f32[256]{0:T(256)S(1)} %add_rsqrt_fusion, f32[2048]{0:T(1024)S(1)} %dynamic_slice.10, pred[]{:T(512)S(6)} %eq.8, pred[]{:T(512)S(6)} %eq.9, f32[256,2048]{1,0:T(8,128)S(1)} %copy-done, ...), kind=kLoop, calls=%fused_computation.19 | loop fusion | flops 4194304 | bytes 12593154 | tf_op jit(solution)/shard_map/jit(_where)/select_n | solution.py:11
  254.9 0.0 all-reduce.6.cloned.1.call-update
  254.9 125.0 %all-reduce.6.cloned.1.call-done = (f32[256,2048]{1,0:T(8,128)}, f32[256,2048]{1,0:T(8,128)}, f32[256,2048]{1,0:T(8,128)}, f32[256,2048]{1,0:T(8,128)}) async-done(((f32[256,2048]{1,0:T(8,128)}, f32[256,2048]{1,0:T(8,128)}, f32[256,2048]{1,0:T(8,128)}, f32[256,2048]{1,0:T(8,128)}), (f32[256,2048]{1,0:T(8,128)}, f32[256,2048]{1,0:T(8,128)}, f32[256,2048]{1,0:T(8,128)}, ...) | async-done | bytes 8388624 | tf_op jit(solution)/shard_map/psum | solution.py:12
  380.0 32.2 %fusion = f32[2048,4096]{1,0:T(8,128)} fusion(f32[256,2048]{1,0:T(8,128)} %get-tuple-element.7, f32[256,2048]{1,0:T(8,128)} %get-tuple-element.8, f32[256,2048]{1,0:T(8,128)S(1)} %copy-done, f32[2048]{0:T(1024)S(1)} %dynamic_slice.10, f32[256]{0:T(256)S(1)} %add_rsqrt_fusion.1), kind=kOutput, calls=%fused_computation.1 | convolution fusion | flops 25771900928 | bytes 39855104 | tf_op jit(solution)/shard_map/dot_general | solution.py:16
  412.2 45.6 %multiply_add_fusion = f32[2048,4096]{1,0:T(8,128)} fusion(f32[2048,4096]{1,0:T(8,128)} %param.9, f32[2048,4096]{1,0:T(8,128)} %fusion, f32[256,2048]{1,0:T(8,128)} %get-tuple-element.9, f32[256,2048]{1,0:T(8,128)} %get-tuple-element.10, f32[256,2048]{1,0:T(8,128)} %get-tuple-element.12, f32[256]{0:T(256)S(1)} %add_rsqrt_fusion, f32[2048]{0:T(1024)S(1)} %dynamic_slice.10), kind=kOutput, calls=%fused_computation | convolution fusion | flops 25797066752 | bytes 106963968 | tf_op jit(solution)/shard_map/dot_general | solution.py:16
  (2 shorter events, 0.0 us)
Async XLA Ops:
  6.5 32.0 %all-gather.7.cloned.1.call-start = ((), (), s32[]{:S(2)}) async-start(), calls=%async_computation.1 | async-start | bytes 2359296 | tf_op jit(solution)/shard_map/all_gather | solution.py:41
  8.4 59.9 %all-gather.5.cloned.1.call-start = ((), (), s32[]{:S(2)}) async-start(), calls=%async_computation | async-start | bytes 2359296 | tf_op jit(solution)/shard_map/all_gather | solution.py:41
  9.2 225.4 %all-reduce.8.cloned.1.call-start = ((), (), s32[]{:S(2)}) async-start(), calls=%async_computation.3 | async-start | bytes 8388608 | tf_op jit(solution)/shard_map/psum | solution.py:48
  47.3 29.7 %copy-start.3 = (f32[2,64,2048]{2,1,0:T(8,128)S(1)}, f32[2,64,2048]{2,1,0:T(8,128)}, u32[]{:S(2)}) copy-start(f32[2,64,2048]{2,1,0:T(8,128)} %param.7) | copy-start | bytes 3145732
  77.2 1.3 copy-start.2
  78.5 1.3 copy-start.1
  79.9 300.1 %all-reduce.6.cloned.1.call-start = ((), (), s32[]{:S(2)}) async-start(), calls=%async_computation.2 | async-start | bytes 16777216 | tf_op jit(solution)/shard_map/psum | solution.py:12
  234.6 14.9 %copy-start = (f32[256,2048]{1,0:T(8,128)S(1)}, f32[256,2048]{1,0:T(8,128)}, u32[]{:S(2)}) copy-start(f32[256,2048]{1,0:T(8,128)} %get-tuple-element.11) | copy-start | bytes 6291460
Sparse Core Ops, SparseCore 0:
  9.2 29.2 all-gather.6
  40.4 27.7 all-gather.4
  80.0 154.5 all-reduce.7
  255.1 124.8 all-reduce.5
where the time goes:
time: 466 us; the launch traced here: 464 us
  waiting for transfers between devices  330 us (71%)
  matrix products  95.2 us (20%)
  between operations  13.2 us (3%)
  blocking collectives  12.2 us (3%)
  other arithmetic  8.37 us (2%)
  local copies, waits for them, and re-layouts  5.2 us (1%)
    psum x1, waiting for transfers between devices, body(): row_panel = lax.psum(partial_value, 'col')  154 us
    psum x1, waiting for transfers between devices, spread(): return lax.psum(block, axis)  125 us
    dot_general x2, matrix products, outer_sum(): lax.dot_general(left_rows, right_rows, (((0,), (0,)), ((), ())), precisio...  77.8 us
    all_gather x2, waiting for transfers between devices, body(): lax.all_gather(attn_out[block_index], 'row', axis=0, tiled=True)  50.3 us
    dot_general x2, matrix products, body(): jnp.dot(lax.all_gather(attn_out[block_index], 'row', axis=0, tiled=True),...  17.4 us
    psum x1, blocking collectives, body(): panel_sums = lax.psum(jnp.sum(row_panel * row_panel, axis=1), 'row')  12.2 us
  transfers between devices with their start and end apart: 4, of which 4 were waited for; matrix products, arithmetic and copies ran while one was open for 2% of the time, Pallas kernels for 0%

commit v1 on v0

v1 whole, which is shorter than its diff:
```python
import functools

import jax
import jax.numpy as jnp
from jax import lax
from jax.experimental import pallas as pl
from jax.experimental.pallas import tpu as pltpu
from jax.sharding import PartitionSpec as P

epsilon_norm = 1e-05
highest = lax.Precision.HIGHEST
MESH = pl.DeviceIdType.MESH
LOG_TOP = 8.4


def power15(v):
    v2 = v * v
    v3 = v2 * v
    v5 = v3 * v2
    return v5 * v5 * v5


def root15(y):
    y = y.astype(jnp.float32)
    mag = jnp.abs(y)
    safe = jnp.maximum(mag, 1e-37)
    root = jnp.exp2(jnp.log2(safe) * (1.0 / 15.0))
    return jnp.where(mag < 1.5e-37, 0.0, jnp.where(y < 0, -root, root))


def remote(src, dst, send_sem, recv_sem, row, col):
    return pltpu.make_async_remote_copy(
        src_ref=src, dst_ref=dst, send_sem=send_sem, recv_sem=recv_sem,
        device_id=(row, col), device_id_type=MESH)


def gather_kernel(rows, fan, own_ref, out_ref, local_sem, send_sem, fwd_sem, recv_sem):
    me = lax.axis_index("row")
    col = lax.axis_index("col")
    chips = rows // fan
    chip, core = me // fan, me % fan
    barrier = pltpu.get_barrier_semaphore()
    for off in range(1, rows):
        pl.semaphore_signal(barrier, inc=1, device_id=((me + off) % rows, col), device_id_type=MESH)
    pl.semaphore_wait(barrier, rows - 1)
    pending = []
    local = pltpu.make_async_copy(own_ref, out_ref.at[me], local_sem)
    local.start()
    for off in range(1, chips):
        there = ((chip + off) % chips) * fan + core
        copy = remote(own_ref, out_ref.at[me], send_sem.at[off], recv_sem.at[me], there, col)
        copy.start()
        pending.append(copy)
    for other in range(1, fan):
        mate = chip * fan + (core + other) % fan
        copy = remote(own_ref, out_ref.at[me], fwd_sem.at[0, other], recv_sem.at[me], mate, col)
        copy.start()
        pending.append(copy)
    for off in range(1, chips):
        slot = ((chip + chips - off) % chips) * fan + core
        remote(own_ref, out_ref.at[slot], send_sem.at[off], recv_sem.at[slot], me, col).wait_recv()
        for other in range(1, fan):
            mate = chip * fan + (core + other) % fan
            copy = remote(out_ref.at[slot], out_ref.at[slot], fwd_sem.at[off, other], recv_sem.at[slot], mate, col)
            copy.start()
            pending.append(copy)
    for off in range(chips):
        for other in range(1, fan):
            slot = ((chip + chips - off) % chips) * fan + (core + other) % fan
            remote(own_ref, out_ref.at[slot], fwd_sem.at[off, other], recv_sem.at[slot], me, col).wait_recv()
    for copy in pending:
        copy.wait_send()
    local.wait()


def gather_rows(own, rows, fan):
    chips = rows // fan
    return pl.pallas_call(
        functools.partial(gather_kernel, rows, fan),
        out_shape=jax.ShapeDtypeStruct((rows,) + own.shape, own.dtype),
        in_specs=[pl.BlockSpec(memory_space=pltpu.VMEM)],
        out_specs=pl.BlockSpec(memory_space=pltpu.VMEM),
        scratch_shapes=[
            pltpu.SemaphoreType.DMA,
            pltpu.SemaphoreType.DMA((chips,)),
            pltpu.SemaphoreType.DMA((chips, fan)),
            pltpu.SemaphoreType.DMA((rows,)),
        ],
        compiler_params=pltpu.CompilerParams(collective_id=0, has_side_effects=True, vmem_limit_bytes=40 << 20),
        name="gather_rows",
    )(own)


def panel_kernel(rows, cols, fan, part_ref, rp_ref, cp_ref, sums, stat_own, stats,
                 rs_send, rs_recv, st_send, st_recv, ag_send, ag_recv, ring_send, mate_send, cp_recv, loc_sem):
    me = lax.axis_index("row")
    col = lax.axis_index("col")
    chips = rows // fan
    chip, core = me // fan, me % fan
    tokens, width = part_ref.shape
    half = tokens // 2
    model = width * rows
    last = cols - 1
    order = [j ^ (j >> 1) for j in range(chips)]
    ahead = jnp.int32(0)
    behind = jnp.int32(0)
    for j in range(chips):
        ahead = jnp.where(chip == order[j], order[(j + 1) % chips], ahead)
        behind = jnp.where(chip == order[j], order[(j + chips - 1) % chips], behind)
    to_chip = jnp.where(core % 2 == 0, ahead, behind)
    to_row = to_chip * fan + core
    is_source = chip == col
    feeds_ring = to_chip != col

    barrier = pltpu.get_barrier_semaphore()
    for off in range(1, rows):
        pl.semaphore_signal(barrier, inc=1, device_id=((me + off) % rows, col), device_id_type=MESH)

    @pl.when(col > 0)
    def _():
        pl.semaphore_signal(barrier, inc=1, device_id=(me, col - 1), device_id_type=MESH)

    @pl.when(col < last)
    def _():
        pl.semaphore_signal(barrier, inc=1, device_id=(me, col + 1), device_id_type=MESH)

    pl.semaphore_wait(barrier, rows - 1 + jnp.minimum(col, 1) + jnp.minimum(last - col, 1))

    rs_count = rs_send.shape[1]
    rs_rows = half // rs_count

    def rs_copy(d, i, src):
        here = pl.ds(pl.multiple_of(i * rs_rows, rs_rows), rs_rows)
        nxt = jnp.maximum(col - 1, 0) if d == 0 else jnp.minimum(col + 1, last)
        source = part_ref.at[pl.ds(pl.multiple_of(d * half + i * rs_rows, rs_rows), rs_rows)] if src == "part" else sums.at[d, here]
        return remote(source, sums.at[d, here], rs_send.at[d, i], rs_recv.at[d, i], me, nxt)

    def rs_step(i, carry):
        for d in range(2):
            first = last if d == 0 else 0
            end = last - first

            @pl.when(col == first)
            def _(d=d):
                rs_copy(d, i, "part").start()

            @pl.when(col != first)
            def _(d=d, end=end):
                rs_copy(d, i, "sums").wait_recv()
                here = pl.ds(pl.multiple_of(i * rs_rows, rs_rows), rs_rows)
                mine = pl.ds(pl.multiple_of(d * half + i * rs_rows, rs_rows), rs_rows)
                sums[d, here, :] = sums[d, here, :] + part_ref[mine, :]

                @pl.when(col != end)
                def _():
                    rs_copy(d, i, "sums").start()
        return carry

    lax.fori_loop(0, rs_count, rs_step, 0)

    block = 128
    for d in range(2):
        end = 0 if d == 0 else last

        @pl.when(col == end)
        def _(d=d):
            ones = jnp.ones((8, width), jnp.float32)
            for b in range(half // block):
                x = sums[d, b * block:(b + 1) * block, :]
                stat_own[:, b * block:(b + 1) * block] = lax.dot_general(
                    ones, x * x, (((1,), (1,)), ((), ())), precision=highest, preferred_element_type=jnp.float32)
            for off in range(1, rows):
                remote(stat_own, stats.at[off], st_send.at[off], st_recv.at[off], (me + off) % rows, col).start()
            total = stat_own[...]
            for off in range(1, rows):
                remote(stat_own, stats.at[off], st_send.at[off], st_recv.at[off], (me + off) % rows, col).wait_recv()
                total = total + stats[off]
            inverse = lax.rsqrt(total / model + epsilon_norm) * (2.0 ** LOG_TOP / model ** 0.5)
            spread = jnp.full((8, 128), 0.125, jnp.float32)
            for b in range(half // block):
                scale = lax.dot_general(
                    inverse[:, b * block:(b + 1) * block], spread, (((0,), (0,)), ((), ())),
                    precision=highest, preferred_element_type=jnp.float32)

                def code(j, carry, b=b, scale=scale):
                    lanes = pl.ds(pl.multiple_of(j * 128, 128), 128)
                    v = sums[d, b * block:(b + 1) * block, lanes] * scale
                    rp_ref[d * half + b * block:d * half + (b + 1) * block, lanes] = power15(v).astype(jnp.bfloat16)
                    return carry

                lax.fori_loop(0, width // 128, code, 0)
            for off in range(1, rows):
                remote(stat_own, stats.at[off], st_send.at[off], st_recv.at[off], (me + off) % rows, col).wait_send()

    ag_count = ag_send.shape[1]
    ag_rows = half // ag_count

    def span(d, i):
        return pl.ds(pl.multiple_of(d * half + i * ag_rows, ag_rows), ag_rows)

    def ag_copy(d, i):
        nxt = jnp.minimum(col + 1, last) if d == 0 else jnp.maximum(col - 1, 0)
        return remote(rp_ref.at[span(d, i)], rp_ref.at[span(d, i)], ag_send.at[d, i], ag_recv.at[d, i], me, nxt)

    def ring_copy(d, i, from_row):
        src = rp_ref.at[span(d, i)] if from_row else cp_ref.at[core, span(d, i)]
        return remote(src, cp_ref.at[core, span(d, i)], ring_send.at[d, i], cp_recv.at[core, d, i], to_row, col)

    def mate_copy(d, i, other, from_row):
        mate = chip * fan + (core + other) % fan
        src = rp_ref.at[span(d, i)] if from_row else cp_ref.at[core, span(d, i)]
        return remote(src, cp_ref.at[core, span(d, i)], mate_send.at[other, d, i], cp_recv.at[core, d, i], mate, col)

    def local_copy(d, i):
        return pltpu.make_async_copy(rp_ref.at[span(d, i)], cp_ref.at[core, span(d, i)], loc_sem.at[d, i])

    def ag_step(i):
        for d in range(2):
            first = 0 if d == 0 else last
            end = last - first

            @pl.when(col != first)
            def _(d=d):
                ag_copy(d, i).wait_recv()

            @pl.when(col != end)
            def _(d=d):
                ag_copy(d, i).start()

            @pl.when(is_source)
            def _(d=d):
                ring_copy(d, i, True).start()
                local_copy(d, i).start()
                for other in range(1, fan):
                    mate_copy(d, i, other, True).start()

    def ring_step(i):
        for d in range(2):
            @pl.when(jnp.logical_not(is_source))
            def _(d=d):
                ring_copy(d, i, False).wait_recv()

                @pl.when(feeds_ring)
                def _():
                    ring_copy(d, i, False).start()

                for other in range(1, fan):
                    mate_copy(d, i, other, False).start()

    lag = min(2, ag_count)
    for i in range(ag_count + lag):
        if i < ag_count:
            ag_step(i)
        if i >= lag:
            ring_step(i - lag)

    def drain(i, carry):
        for d in range(2):
            rs_first = last if d == 0 else 0
            ag_first = last - rs_first

            @pl.when(col != rs_first)
            def _(d=d):
                pass

            for other in range(1, fan):
                theirs = (core + other) % fan
                remote(rp_ref.at[span(d, i)], cp_ref.at[theirs, span(d, i)], mate_send.at[other, d, i],
                       cp_recv.at[theirs, d, i], me, col).wait_recv()
                mate_copy(d, i, other, True).wait_send()

            @pl.when(col != last - ag_first)
            def _(d=d):
                ag_copy(d, i).wait_send()

            @pl.when(is_source)
            def _(d=d):
                local_copy(d, i).wait()

            @pl.when(jnp.logical_or(is_source, feeds_ring))
            def _(d=d):
                ring_copy(d, i, True).wait_send()
        return carry

    lax.fori_loop(0, ag_count, drain, 0)

    def rs_drain(i, carry):
        for d in range(2):
            end = 0 if d == 0 else last

            @pl.when(col != end)
            def _(d=d):
                rs_copy(d, i, "sums").wait_send()
        return carry

    lax.fori_loop(0, rs_count, rs_drain, 0)


def panels(part, rows, cols, fan):
    tokens, width = part.shape
    half = tokens // 2
    rs_count = half // 16
    ag_count = half // 32
    vmem = pl.BlockSpec(memory_space=pltpu.VMEM)
    dma = pltpu.SemaphoreType.DMA
    return pl.pallas_call(
        functools.partial(panel_kernel, rows, cols, fan),
        out_shape=(
            jax.ShapeDtypeStruct((tokens, width), jnp.bfloat16),
            jax.ShapeDtypeStruct((fan, tokens, width), jnp.bfloat16),
        ),
        in_specs=[vmem],
        out_specs=(vmem, vmem),
        scratch_shapes=[
            pltpu.VMEM((2, half, width), jnp.float32),
            pltpu.VMEM((8, half), jnp.float32),
            pltpu.VMEM((rows, 8, half), jnp.float32),
            dma((2, rs_count)), dma((2, rs_count)),
            dma((rows,)), dma((rows,)),
            dma((2, ag_count)), dma((2, ag_count)),
            dma((2, ag_count)), dma((fan, 2, ag_count)), dma((fan, 2, ag_count)),
            dma((2, ag_count)),
        ],
        compiler_params=pltpu.CompilerParams(collective_id=1, has_side_effects=True, vmem_limit_bytes=48 << 20),
        name="panels",
    )(part)


def split(value):
    high = lax.reduce_precision(value, 8, 7)
    low = value - high
    return high.astype(jnp.bfloat16), low.astype(jnp.bfloat16)


def body(attn_out, o_weight, residual, norm_gain, gram_in):
    rows = lax.axis_size("row")
    cols = lax.axis_size("col")
    fan = rows // cols
    row_index = lax.axis_index("row")
    col_index = lax.axis_index("col")
    groups, tile = attn_out.shape[0], attn_out.shape[1]
    width, model_width = o_weight.shape[1], o_weight.shape[1] * rows
    tokens = groups * tile * rows

    attn = gather_rows(attn_out.reshape(groups * tile, -1), rows, fan).reshape(tokens, -1)
    part = jnp.dot(attn, o_weight, preferred_element_type=jnp.float32)
    mine = residual.reshape(groups, fan, tile, width).transpose(1, 0, 2, 3).reshape(-1, width)
    offset = col_index * mine.shape[0]
    own = lax.dynamic_slice_in_dim(part, offset, mine.shape[0], 0) + mine
    part = lax.dynamic_update_slice_in_dim(part, own, offset, 0)
    row_code, col_code = panels(part, rows, cols, fan)

    unit = model_width ** 0.5 / 2.0 ** LOG_TOP
    gain_rows = lax.dynamic_slice_in_dim(norm_gain, row_index * width, width) * (unit / tokens)
    gain_cols = (lax.dynamic_slice_in_dim(norm_gain, col_index * fan * width, fan * width) * unit).reshape(fan, 1, width)
    lh, ll = split(root15(row_code) * gain_rows[None, :])
    rh, rl = split(root15(col_code) * gain_cols)
    left = jnp.concatenate([lh, lh, ll], axis=0)
    right = jnp.concatenate([rh, rl, rh], axis=1)
    gram = lax.dot_general(
        left, right.transpose(1, 0, 2).reshape(3 * tokens, fan * width), (((0,), (0,)), ((), ())),
        preferred_element_type=jnp.float32)
    return gram_in + gram


def solution(mesh):
    return jax.shard_map(
        body,
        mesh=mesh,
        in_specs=(
            P(None, "row", "col"),
            P("col", "row"),
            P(None, "col", "row"),
            P(),
            P("row", "col"),
        ),
        out_specs=P("row", "col"),
        check_vma=False,
    )
```

time: 466 us -> 741 us (1.59)
  Pallas kernels: 0 us -> 641 us
  waiting for transfers between devices: 330 us -> 0 us
  matrix products: 95.2 us -> 47.9 us
  other arithmetic: 8.37 us -> 30.6 us
  local copies, waits for them, and re-layouts: 5.2 us -> 21 us
  between operations: 13.2 us -> 0.08 us
  blocking collectives: 12.2 us -> 0 us
    pallas_call x0 -> x2, Pallas kernels: none -> 641 us  [the longest x1 611 us: panels(): pl.pallas_call(functools.partial(panel_kernel, rows, cols, fan), out_shap...]
    psum x2 -> x0, waiting for transfers between devices: 279 us -> none  [the longest x1 154 us: body(): row_panel = lax.psum(partial_value, 'col')]
    all_gather x2 -> x0, waiting for transfers between devices: 50.3 us -> none  [body(): lax.all_gather(attn_out[block_index], 'row', axis=0, tiled=True)]
    dot_general x4 -> x2, matrix products: 95.2 us -> 47.9 us  [the longest x1 36.3 us: body(): lax.dot_general(left, right.transpose(1, 0, 2).reshape(3 * tokens, fan *...]
    transpose x0 -> x1, other arithmetic: none -> 20.7 us  [body(): right.transpose(1, 0, 2).reshape(3 * tokens, fan * width)]
    transpose x0 -> x1, local copies, waits for them, and re-layouts: none -> 16.6 us  [body(): right.transpose(1, 0, 2).reshape(3 * tokens, fan * width)]
    psum x1 -> x0, blocking collectives: 12.2 us -> none  [body(): panel_sums = lax.psum(jnp.sum(row_panel * row_panel, axis=1), 'row')]
    convert_element_type x0 -> x2, other arithmetic: none -> 8.37 us  [split(): return (high.astype(jnp.bfloat16), low.astype(jnp.bfloat16))]
  transfers between devices with their start and end apart: 4 -> 0, of which waited for: 4 -> 0; matrix products, arithmetic and copies ran while one was open for 2% -> 0% of each run, Pallas kernels for 0% -> 0%
where the time goes in v1:
time: 741 us
  Pallas kernels  641 us (87%)
  matrix products  47.9 us (6%)
  other arithmetic  30.6 us (4%)
  local copies, waits for them, and re-layouts  21 us (3%)
    pallas_call x1, Pallas kernels, panels(): pl.pallas_call(functools.partial(panel_kernel, rows, cols, fan), out_shap...  611 us
    dot_general x1, matrix products, body(): lax.dot_general(left, right.transpose(1, 0, 2).reshape(3 * tokens, fan *...  36.3 us
    pallas_call x1, Pallas kernels, gather_rows(): pl.pallas_call(functools.partial(gather_kernel, rows, fan), out_shape=jax...  29.5 us
    transpose x1, other arithmetic, body(): right.transpose(1, 0, 2).reshape(3 * tokens, fan * width)  20.7 us
    transpose x1, local copies, waits for them, and re-layouts, body(): right.transpose(1, 0, 2).reshape(3 * tokens, fan * width)  16.6 us

profile of v1, /device:TPU:5, one launch (start us, length us, event | category | flops | bytes accessed | tf_op | source)
XLA Modules:
  0.0 740.5 jit_solution(11477823148977404503)
XLA Ops:
  0.0 0.7 dynamic-slice_multiply_fusion.1
  0.7 0.7 dynamic-slice_multiply_fusion
  1.4 1.3 copy.7
  2.8 0.0 copy-start
  2.8 1.0 copy-done
  3.8 29.5 %gather_rows.1 = bf16[8,64,4096]{2,1,0:T(8,128)(2,1)S(1)} custom-call(bf16[64,4096]{1,0:T(8,128)(2,1)S(1)} %bitcast.14), custom_call_target="tpu_custom_call" | custom-call | tf_op jit(solution)/shard_map/gather_rows/pallas_call | solution.py:78
  33.3 11.5 %fusion.22 = f32[512,2048]{1,0:T(8,128)S(1)} fusion(bf16[512,4096]{1,0:T(8,128)(2,1)S(1)} %bitcast.13, bf16[4096,2048]{1,0:T(8,128)(2,1)} %param.6), kind=kOutput, calls=%fused_computation.38 | convolution fusion | flops 8589934592 | bytes 25165824 | tf_op jit(solution)/shard_map/dot_general | solution.py:346
  44.8 0.2 constant_dynamic-update-slice_fusion.part_ref
  45.0 0.0 copy-start.1
  45.0 2.0 copy-done.1
  47.0 611.5 %panels.1 = (bf16[512,2048]{1,0:T(8,128)(2,1)S(1)}, bf16[2,512,2048]{2,1,0:T(8,128)(2,1)}) custom-call(f32[512,2048]{1,0:T(8,128)} %copy-done.1), custom_call_target="tpu_custom_call" | custom-call | tf_op jit(solution)/shard_map/panels/pallas_call | solution.py:306
  658.5 0.0 copy-start.2
  658.5 3.5 reduce-precision_convert_fusion.1
  662.0 0.0 copy-done.2
  662.0 4.9 fusion.5
  666.9 20.7 %maximum_bitcast_fusion = bf16[1536,2,2048]{2,0,1:T(8,128)(2,1)} fusion(bf16[2,512,2048]{2,1,0:T(8,128)(2,1)S(1)} %get-tuple-element.10, bf16[2,512,2048]{2,1,0:T(8,128)(2,1)S(1)} %get-tuple-element.9), kind=kLoop, calls=%fused_computation.1 | loop fusion | flops 37748736 | bytes 20971520 | tf_op jit(solution)/shard_map/transpose | solution.py:361
  687.6 16.6 %copy.8 = bf16[1536,2,2048]{0,2,1:T(8,128)(2,1)} copy(bf16[1536,2,2048]{2,0,1:T(8,128)(2,1)} %maximum_bitcast_fusion) | data formatting | bytes 25165824 | tf_op jit(solution)/shard_map/transpose | solution.py:361
  704.2 36.3 %convolution_add_fusion = f32[2048,4096]{1,0:T(8,128)} fusion(f32[2048,4096]{1,0:T(8,128)} %param.9, bf16[1536,4096]{0,1:T(8,128)(2,1)} %bitcast.15, bf16[512,2048]{1,0:T(8,128)(2,1)} %get-tuple-element.12, bf16[512,2048]{1,0:T(8,128)(2,1)S(1)} %get-tuple-element.11), kind=kOutput, calls=%fused_computation | convolution fusion | flops 25797066752 | bytes 83886080 | tf_op jit(solution)/shard_map/dot_general | solution.py:360
  (1 shorter events, 0.0 us)
Async XLA Ops:
  2.8 1.0 copy-start
  45.0 2.0 copy-start.1
  658.5 3.5 copy-start.2

commit v2 on v1

--- a/solution.py
+++ b/solution.py
@@ -104,13 +104,19 @@
     order = [j ^ (j >> 1) for j in range(chips)]
     ahead = jnp.int32(0)
     behind = jnp.int32(0)
+    spot = jnp.int32(0)
+    source_spot = jnp.int32(0)
     for j in range(chips):
+        spot = jnp.where(chip == order[j], j, spot)
+        source_spot = jnp.where(col == order[j], j, source_spot)
         ahead = jnp.where(chip == order[j], order[(j + 1) % chips], ahead)
         behind = jnp.where(chip == order[j], order[(j + chips - 1) % chips], behind)
     to_chip = jnp.where(core % 2 == 0, ahead, behind)
     to_row = to_chip * fan + core
     is_source = chip == col
     feeds_ring = to_chip != col
+    turn = jnp.where(core % 2 == 0, spot - source_spot, source_spot - spot)
+    ring_hops = (turn + chips) % chips
 
     barrier = pltpu.get_barrier_semaphore()
     for off in range(1, rows):
@@ -135,17 +141,23 @@
         source = part_ref.at[pl.ds(pl.multiple_of(d * half + i * rs_rows, rs_rows), rs_rows)] if src == "part" else sums.at[d, here]
         return remote(source, sums.at[d, here], rs_send.at[d, i], rs_recv.at[d, i], me, nxt)
 
-    def rs_step(i, carry):
+    for d in range(2):
+        @pl.when(col == (last if d == 0 else 0))
+        def _(d=d):
+            def send_all(i, carry):
+                rs_copy(d, i, "part").start()
+                return carry
+
+            lax.fori_loop(0, rs_count, send_all, 0)
+
+    def rs_step(s, carry):
         for d in range(2):
-            first = last if d == 0 else 0
-            end = last - first
-
-            @pl.when(col == first)
-            def _(d=d):
-                rs_copy(d, i, "part").start()
-
-            @pl.when(col != first)
-            def _(d=d, end=end):
+            end = 0 if d == 0 else last
+            hops = last - col if d == 0 else col
+            i = s - hops
+
+            @pl.when(jnp.logical_and(hops > 0, jnp.logical_and(i >= 0, i < rs_count)))
+            def _(d=d, end=end, i=i):
                 rs_copy(d, i, "sums").wait_recv()
                 here = pl.ds(pl.multiple_of(i * rs_rows, rs_rows), rs_rows)
                 mine = pl.ds(pl.multiple_of(d * half + i * rs_rows, rs_rows), rs_rows)
@@ -156,7 +168,7 @@
                     rs_copy(d, i, "sums").start()
         return carry
 
-    lax.fori_loop(0, rs_count, rs_step, 0)
+    lax.fori_loop(1, rs_count + last, rs_step, 0)
 
     block = 128
     for d in range(2):
@@ -198,46 +210,64 @@
     def span(d, i):
         return pl.ds(pl.multiple_of(d * half + i * ag_rows, ag_rows), ag_rows)
 
+    def lanes(which):
+        return pl.ds(pl.multiple_of(which * width, width), width)
+
     def ag_copy(d, i):
         nxt = jnp.minimum(col + 1, last) if d == 0 else jnp.maximum(col - 1, 0)
         return remote(rp_ref.at[span(d, i)], rp_ref.at[span(d, i)], ag_send.at[d, i], ag_recv.at[d, i], me, nxt)
 
     def ring_copy(d, i, from_row):
-        src = rp_ref.at[span(d, i)] if from_row else cp_ref.at[core, span(d, i)]
-        return remote(src, cp_ref.at[core, span(d, i)], ring_send.at[d, i], cp_recv.at[core, d, i], to_row, col)
+        src = rp_ref.at[span(d, i)] if from_row else cp_ref.at[span(d, i), lanes(core)]
+        return remote(src, cp_ref.at[span(d, i), lanes(core)], ring_send.at[d, i], cp_recv.at[core, d, i], to_row, col)
 
     def mate_copy(d, i, other, from_row):
         mate = chip * fan + (core + other) % fan
-        src = rp_ref.at[span(d, i)] if from_row else cp_ref.at[core, span(d, i)]
-        return remote(src, cp_ref.at[core, span(d, i)], mate_send.at[other, d, i], cp_recv.at[core, d, i], mate, col)
+        src = rp_ref.at[span(d, i)] if from_row else cp_ref.at[span(d, i), lanes(core)]
+        return remote(src, cp_ref.at[span(d, i), lanes(core)], mate_send.at[other, d, i], cp_recv.at[core, d, i], mate, col)
 
     def local_copy(d, i):
-        return pltpu.make_async_copy(rp_ref.at[span(d, i)], cp_ref.at[core, span(d, i)], loc_sem.at[d, i])
-
-    def ag_step(i):
+        return pltpu.make_async_copy(rp_ref.at[span(d, i)], cp_ref.at[span(d, i), lanes(core)], loc_sem.at[d, i])
+
+    def have_panel(d, i):
+        end = last if d == 0 else 0
+
+        @pl.when(col != end)
+        def _():
+            ag_copy(d, i).start()
+
+        @pl.when(is_source)
+        def _():
+            ring_copy(d, i, True).start()
+            local_copy(d, i).start()
+            for other in range(1, fan):
+                mate_copy(d, i, other, True).start()
+
+    for d in range(2):
+        @pl.when(col == (0 if d == 0 else last))
+        def _(d=d):
+            def send_all(i, carry):
+                have_panel(d, i)
+                return carry
+
+            lax.fori_loop(0, ag_count, send_all, 0)
+
+    def ag_step(s, carry):
         for d in range(2):
-            first = 0 if d == 0 else last
-            end = last - first
-
-            @pl.when(col != first)
-            def _(d=d):
+            hops = col if d == 0 else last - col
+            i = s - hops
+
+            @pl.when(jnp.logical_and(hops > 0, jnp.logical_and(i >= 0, i < ag_count)))
+            def _(d=d, i=i):
                 ag_copy(d, i).wait_recv()
-
-            @pl.when(col != end)
-            def _(d=d):
-                ag_copy(d, i).start()
-
-            @pl.when(is_source)
-            def _(d=d):
-                ring_copy(d, i, True).start()
-                local_copy(d, i).start()
-                for other in range(1, fan):
-                    mate_copy(d, i, other, True).start()
-
-    def ring_step(i):
+                have_panel(d, i)
+
         for d in range(2):
-            @pl.when(jnp.logical_not(is_source))
-            def _(d=d):
+            hops = (col if d == 0 else last - col) + ring_hops
+            i = s - hops
+
+            @pl.when(jnp.logical_and(ring_hops > 0, jnp.logical_and(i >= 0, i < ag_count)))
+            def _(d=d, i=i):
                 ring_copy(d, i, False).wait_recv()
 
                 @pl.when(feeds_ring)
@@ -246,26 +276,18 @@
 
                 for other in range(1, fan):
                     mate_copy(d, i, other, False).start()
-
-    lag = min(2, ag_count)
-    for i in range(ag_count + lag):
-        if i < ag_count:
-            ag_step(i)
-        if i >= lag:
-            ring_step(i - lag)
+        return carry
+
+    lax.fori_loop(1, ag_count + last + chips - 1, ag_step, 0)
 
     def drain(i, carry):
         for d in range(2):
             rs_first = last if d == 0 else 0
             ag_first = last - rs_first
 
-            @pl.when(col != rs_first)
-            def _(d=d):
-                pass
-
             for other in range(1, fan):
                 theirs = (core + other) % fan
-                remote(rp_ref.at[span(d, i)], cp_ref.at[theirs, span(d, i)], mate_send.at[other, d, i],
+                remote(rp_ref.at[span(d, i)], cp_ref.at[span(d, i), lanes(theirs)], mate_send.at[other, d, i],
                        cp_recv.at[theirs, d, i], me, col).wait_recv()
                 mate_copy(d, i, other, True).wait_send()
 
@@ -307,7 +329,7 @@
         functools.partial(panel_kernel, rows, cols, fan),
         out_shape=(
             jax.ShapeDtypeStruct((tokens, width), jnp.bfloat16),
-            jax.ShapeDtypeStruct((fan, tokens, width), jnp.bfloat16),
+            jax.ShapeDtypeStruct((tokens, fan * width), jnp.bfloat16),
         ),
         in_specs=[vmem],
         out_specs=(vmem, vmem),
@@ -352,13 +374,13 @@
 
     unit = model_width ** 0.5 / 2.0 ** LOG_TOP
     gain_rows = lax.dynamic_slice_in_dim(norm_gain, row_index * width, width) * (unit / tokens)
-    gain_cols = (lax.dynamic_slice_in_dim(norm_gain, col_index * fan * width, fan * width) * unit).reshape(fan, 1, width)
+    gain_cols = (lax.dynamic_slice_in_dim(norm_gain, col_index * fan * width, fan * width) * unit)[None, :]
     lh, ll = split(root15(row_code) * gain_rows[None, :])
     rh, rl = split(root15(col_code) * gain_cols)
     left = jnp.concatenate([lh, lh, ll], axis=0)
-    right = jnp.concatenate([rh, rl, rh], axis=1)
+    right = jnp.concatenate([rh, rl, rh], axis=0)
     gram = lax.dot_general(
-        left, right.transpose(1, 0, 2).reshape(3 * tokens, fan * width), (((0,), (0,)), ((), ())),
+        left, right, (((0,), (0,)), ((), ())),
         preferred_element_type=jnp.float32)
     return gram_in + gram
 

time: 741 us -> 222 us (0.30)
  Pallas kernels: 641 us -> 157 us
  other arithmetic: 30.6 us -> 12 us
  local copies, waits for them, and re-layouts: 21 us -> 4.36 us
    pallas_call x1, Pallas kernels: 611 us -> 128 us  [panels(): pl.pallas_call(functools.partial(panel_kernel, rows, cols, fan), out_shap...]
    transpose x1 -> x0, other arithmetic: 20.7 us -> none  [body(): right.transpose(1, 0, 2).reshape(3 * tokens, fan * width)]
    transpose x1 -> x0, local copies, waits for them, and re-layouts: 16.6 us -> none  [body(): right.transpose(1, 0, 2).reshape(3 * tokens, fan * width)]
where the time goes in v2:
time: 222 us; the launch traced here: 221 us
  Pallas kernels  157 us (71%)
  matrix products  47.9 us (22%)
  other arithmetic  12 us (5%)
  local copies, waits for them, and re-layouts  4.36 us (2%)
    pallas_call x1, Pallas kernels, panels(): pl.pallas_call(functools.partial(panel_kernel, rows, cols, fan), out_shap...  128 us
    dot_general x1, matrix products, body(): lax.dot_general(left, right, (((0,), (0,)), ((), ())), preferred_element_...  36.4 us
    pallas_call x1, Pallas kernels, gather_rows(): pl.pallas_call(functools.partial(gather_kernel, rows, fan), out_shape=jax...  29.5 us
    dot_general x1, matrix products, body(): part = jnp.dot(attn, o_weight, preferred_element_type=jnp.float32)  11.5 us
    convert_element_type x2, other arithmetic, split(): return (high.astype(jnp.bfloat16), low.astype(jnp.bfloat16))  10.4 us

profile of v2, /device:TPU:5, one launch (start us, length us, event | category | flops | bytes accessed | tf_op | source)
XLA Modules:
  0.0 221.5 jit_solution(6403523290509561894)
XLA Ops:
  0.0 0.7 dynamic-slice_multiply_fusion.1
  0.7 0.7 dynamic-slice_multiply_fusion
  1.4 1.3 copy.6
  2.7 0.0 copy-start
  2.8 1.0 copy-done
  3.8 29.5 %gather_rows.1 = bf16[8,64,4096]{2,1,0:T(8,128)(2,1)S(1)} custom-call(bf16[64,4096]{1,0:T(8,128)(2,1)S(1)} %bitcast.10), custom_call_target="tpu_custom_call" | custom-call | tf_op jit(solution)/shard_map/gather_rows/pallas_call | solution.py:78
  33.3 11.5 %fusion.27 = f32[512,2048]{1,0:T(8,128)S(1)} fusion(bf16[512,4096]{1,0:T(8,128)(2,1)S(1)} %bitcast.9, bf16[4096,2048]{1,0:T(8,128)(2,1)} %param.6), kind=kOutput, calls=%fused_computation.42 | convolution fusion | flops 8589934592 | bytes 25165824 | tf_op jit(solution)/shard_map/dot_general | solution.py:368
  44.8 0.2 constant_dynamic-update-slice_fusion.part_ref
  45.0 0.0 copy-start.1
  45.0 2.0 copy-done.1
  47.0 127.6 %panels.1 = (bf16[512,2048]{1,0:T(8,128)(2,1)S(1)}, bf16[512,4096]{1,0:T(8,128)(2,1)}) custom-call(f32[512,2048]{1,0:T(8,128)} %copy-done.1), custom_call_target="tpu_custom_call" | custom-call | tf_op jit(solution)/shard_map/panels/pallas_call | solution.py:328
  174.7 0.0 copy-start.2
  174.7 3.6 %reduce-precision_convert_fusion.1 = (bf16[512,2048]{1,0:T(8,128)(2,1)S(1)}, bf16[512,2048]{1,0:T(8,128)(2,1)}) fusion(bf16[512,2048]{1,0:T(8,128)(2,1)S(1)} %get-tuple-element.7, f32[2048]{0:T(1024)S(1)} %dynamic-slice_multiply_fusion.1), kind=kLoop, calls=%fused_computation.26 | loop fusion | flops 14680064 | bytes 6299648 | tf_op jit(solution)/shard_map/convert_element_type | solution.py:354
  178.2 0.0 copy-done.2
  178.2 6.8 %fusion.10 = (bf16[512,4096]{1,0:T(8,128)(2,1)}, bf16[512,4096]{1,0:T(8,128)(2,1)}) fusion(bf16[512,4096]{1,0:T(8,128)(2,1)S(1)} %copy-done.2, f32[4096]{0:T(1024)S(1)} %dynamic-slice_multiply_fusion), kind=kLoop, calls=%fused_computation.16 | loop fusion | flops 29360128 | bytes 12599296 | tf_op jit(solution)/shard_map/convert_element_type | solution.py:354
  185.1 36.4 %convolution_add_fusion = f32[2048,4096]{1,0:T(8,128)} fusion(f32[2048,4096]{1,0:T(8,128)} %param.9, bf16[512,4096]{1,0:T(8,128)(2,1)} %get-tuple-element.10, bf16[512,4096]{1,0:T(8,128)(2,1)} %get-tuple-element.9, bf16[512,2048]{1,0:T(8,128)(2,1)} %get-tuple-element.12, bf16[512,2048]{1,0:T(8,128)(2,1)S(1)} %get-tuple-element.11), kind=kOutput, calls=%fused_computation | convolution fusion | flops 25834815488 | bytes 79691776 | tf_op jit(solution)/shard_map/dot_general | solution.py:382
Async XLA Ops:
  2.7 1.0 copy-start
  45.0 2.0 copy-start.1
  174.7 3.6 %copy-start.2 = (bf16[512,4096]{1,0:T(8,128)(2,1)S(1)}, bf16[512,4096]{1,0:T(8,128)(2,1)}, u32[]{:S(2)}) copy-start(bf16[512,4096]{1,0:T(8,128)(2,1)} %get-tuple-element.8) | copy-start | bytes 12582916
